TPU v7x, 256 devices: a whole 4x4x8 slice. The times are simulated.
256 devices in a mesh: lat: 2 (over x_hi), dp: 64 (over z, y, core), exp: 2 (over x_lo).
Axes of the slice: x: 4 (x_hi: 2, x_lo: 2; x = x_hi * 2 + x_lo), y: 4, z: 8, core: 2. Of those that a mesh axis runs over, the one named last changes fastest.
Arguments:
- images: bfloat16 [128, 32, 256, 192], P(('dp', 'exp'), 'lat'), may hold values from -6 to 6
- cotangent: bfloat16 [128, 32, 256, 192], P(('dp', 'exp'), 'lat'), may hold values from -0.0625 to 0.0625
- labels: int32 [128, 32, 2, 1], P(('dp', 'exp'), 'lat'), may hold values from 0 to 15; in each aligned block of 32 rows (0 to 31, 32 to 63, ..., all dimensions but the last counted through in order) at most 3 rows name the same one
- dw_kernel: float32 [7, 7, 192], replicated, may hold values from -0.875 to 0.875
- ln_gain: float32 [192], replicated, may hold values from 0.5 to 2
- w_expand: bfloat16 [192, 768], replicated, may hold values from -0.4375 to 0.4375
- w_reduce: bfloat16 [768, 192], replicated, may hold values from -0.21875 to 0.21875
- exp_in: bfloat16 [16, 192, 768], P('exp'), may hold values from -0.4375 to 0.4375
- exp_out: bfloat16 [16, 768, 192], P('exp'), may hold values from -0.21875 to 0.21875
Outputs:
- output: bfloat16 [128, 32, 256, 192], P(('dp', 'exp'), 'lat')
- grad_in: float32 [16, 192, 768], P('exp')
- grad_out: float32 [16, 768, 192], P('exp')
Inputs may be any that keep to these rules, and one draw needn't show every extreme that they name: `labels`: among the 32 row blocks of one device (aligned runs of 32 blocks in the order clip, row, block), no class is named more than 3 times, a bound that some block reaches.
All inputs are finite; a program needn't handle non-finite values.
Results may differ from a plain program's by a relative error of at most 0.0072.
Values may be sent and summed in bfloat16 or wider, within the bound.
A program may use at most 128 MiB of HBM per device.

v0:
```python
import jax
import jax.numpy as jnp
from jax import lax
from jax.sharding import PartitionSpec as P

EXPERTS = 16
BLOCK = 128
CAP = 3


def with_halo(block, sides, width):
    for axis, dim in sides:
        count = lax.axis_size(axis)
        forward = [(i, i + 1) for i in range(count - 1)]
        backward = [(target, source) for source, target in forward]
        low = lax.ppermute(
            lax.slice_in_dim(block, block.shape[dim] - width, None, axis=dim), axis, forward
        )
        high = lax.ppermute(lax.slice_in_dim(block, 0, width, axis=dim), axis, backward)
        block = jnp.concatenate([low, block, high], axis=dim)
    return block


def gelu_slope(values):
    return (
        0.5 * (1.0 + lax.erf(values * 0.7071067811865476))
        + values * jnp.exp(-0.5 * values * values) * 0.3989422804014327
    )


def depthwise(padded, kernel):
    row_count = padded.shape[1] - 6
    col_count = padded.shape[2] - 6
    summed = jnp.zeros((padded.shape[0], row_count, col_count, padded.shape[3]), jnp.float32)
    for row_off in range(7):
        for col_off in range(7):
            window = padded[:, row_off : row_off + row_count, col_off : col_off + col_count, :]
            summed = summed + window.astype(jnp.float32) * kernel[row_off, col_off]
    return summed


def widen(picture):
    return jnp.pad(picture, ((0, 0), (0, 0), (3, 3), (0, 0)))


def dense_block(images, smoothed, ln_gain, w_expand, w_reduce):
    channels = images.shape[-1]
    channel_mean = jnp.mean(smoothed, axis=-1, keepdims=True)
    centered = smoothed - channel_mean
    variance = jnp.mean(centered * centered, axis=-1, keepdims=True)
    normed = (centered * lax.rsqrt(variance + 1e-06) * ln_gain).astype(jnp.bfloat16)
    flat_normed = normed.reshape(-1, channels)
    expanded = jnp.dot(flat_normed, w_expand, preferred_element_type=jnp.float32)
    active = jax.nn.gelu(expanded, approximate=False).astype(jnp.bfloat16)
    reduced = jnp.dot(active, w_reduce, preferred_element_type=jnp.float32)
    dense_out = images.reshape(-1, channels).astype(jnp.float32) + reduced
    return dense_out.astype(jnp.bfloat16).reshape(images.shape)


def expert_pass(inputs, grads_in, w_in, w_out):
    pre_act = jnp.dot(inputs, w_in, preferred_element_type=jnp.float32)
    hidden = jax.nn.gelu(pre_act, approximate=False).astype(jnp.bfloat16)
    outputs = jnp.dot(hidden, w_out, preferred_element_type=jnp.float32).astype(jnp.bfloat16)
    grad_out = jnp.dot(hidden.T, grads_in, preferred_element_type=jnp.float32)
    back_prop = jnp.dot(grads_in, w_out.T, preferred_element_type=jnp.float32)
    scaled = (back_prop * gelu_slope(pre_act)).astype(jnp.bfloat16)
    grad_in = jnp.dot(inputs.T, scaled, preferred_element_type=jnp.float32)
    return (outputs, grad_in, grad_out)


def body(images, cotangent, labels, dw_kernel, ln_gain, w_expand, w_reduce, exp_in, exp_out):
    channels = images.shape[-1]
    padded = with_halo(images, (("lat", 1),), 3)
    smoothed = depthwise(widen(padded), dw_kernel)
    dense_out = dense_block(images, smoothed, ln_gain, w_expand, w_reduce)
    block_width = BLOCK * channels
    blocks = dense_out.reshape(-1, block_width)
    grad_blocks = cotangent.reshape(-1, block_width)
    flat_labels = labels.reshape(-1)
    members = (flat_labels[:, None] == jnp.arange(EXPERTS, dtype=jnp.int32)[None, :]).astype(
        jnp.int32
    )
    before = jnp.sum(jnp.cumsum(members, axis=0) * members, axis=1) - 1
    slot_of = flat_labels * CAP + before
    placer = (jnp.arange(EXPERTS * CAP, dtype=jnp.int32)[:, None] == slot_of[None, :]).astype(
        jnp.bfloat16
    )
    outgoing = (
        jnp.dot(placer, blocks, preferred_element_type=jnp.float32)
        .astype(jnp.bfloat16)
        .reshape(EXPERTS, CAP, block_width)
    )
    outgoing_grads = (
        jnp.dot(placer, grad_blocks, preferred_element_type=jnp.float32)
        .astype(jnp.bfloat16)
        .reshape(EXPERTS, CAP, block_width)
    )

    def run_expert(expert_items):
        inputs, grads_in, w_in, w_out = expert_items
        outputs, grad_in, grad_out = expert_pass(
            inputs.reshape(-1, channels), grads_in.reshape(-1, channels), w_in, w_out
        )
        return (outputs.reshape(inputs.shape), grad_in, grad_out)

    arrived, arrived_grads = (
        lax.all_to_all(outgoing, "exp", split_axis=0, concat_axis=1, tiled=True),
        lax.all_to_all(outgoing_grads, "exp", split_axis=0, concat_axis=1, tiled=True),
    )
    results, grad_in, grad_out = lax.map(run_expert, (arrived, arrived_grads, exp_in, exp_out))
    returned = lax.all_to_all(results, "exp", split_axis=1, concat_axis=0, tiled=True)
    grad_in, grad_out = lax.psum((grad_in, grad_out), ("lat", "dp"))
    expert_out = jnp.dot(
        placer.T, returned.reshape(EXPERTS * CAP, block_width), preferred_element_type=jnp.float32
    ).astype(jnp.bfloat16)
    output = (
        dense_out.astype(jnp.float32) + expert_out.reshape(dense_out.shape).astype(jnp.float32)
    ).astype(jnp.bfloat16)
    return (output, grad_in, grad_out)


def solution(mesh):
    in_specs = (
        P(("dp", "exp"), "lat", None, None),
        P(("dp", "exp"), "lat", None, None),
        P(("dp", "exp"), "lat", None, None),
        P(),
        P(),
        P(),
        P(),
        P("exp", None, None),
        P("exp", None, None),
    )
    out_specs = (P(("dp", "exp"), "lat", None, None), P("exp", None, None), P("exp", None, None))
    return jax.shard_map(body, mesh=mesh, in_specs=in_specs, out_specs=out_specs, check_vma=False)
```

profile of v0, /device:TPU:2, one launch (start us, length us, event | category | flops | bytes accessed | tf_op | source)
XLA Modules:
  0.0 1631.7 jit_solution(9651882044922824037)
XLA Ops:
  9.0 4.0 collective-permute-start
  18.3 3.2 reshape.261
  26.1 6.8 all-to-all-start.1
  38.0 26.9 %fusion.104 = (f32[16,256]{1,0:T(8,128)S(1)}, f32[1,16,256,192]{2,3,1,0:T(8,128)S(1)}) fusion(f32[192]{0:T(256)S(1)} %bitcast.170, bf16[1,22,262,192]{2,3,1,0:T(8,128)(2,1)S(1)} %fusion.69, f32[192]{0:T(256)S(1)} %bitcast.171, f32[192]{0:T(256)S(1)} %bitcast.143, f32[192]{0:T(256)S(1)} %bitcast.144, ...), kind=kLoop, calls=%fused_computation.138 | loop fusion | flops 115601408 | bytes 80270080 | tf_op jit(solution)/shard_map/reduce_sum | solution.py:48
  68.0 42.4 %fusion.60 = bf16[4096,192]{0,1:T(8,128)(2,1)} fusion(f32[4096,192]{0,1:T(8,128)S(1)} %bitcast.140, bf16[768,192]{0,1:T(8,128)(2,1)S(1)} %copy-done, bf16[4096,192]{0,1:T(8,128)(2,1)} %bitcast.141, bf16[192,768]{1,0:T(8,128)(2,1)} %param.16), kind=kOutput, calls=%fused_computation.83 | convolution fusion | flops 2621964288 | bytes 6881280 | tf_op jit(solution)/shard_map/dot_general | solution.py:55
  121.4 4.0 all-to-all-start
  125.4 3.6 copy.25
  131.9 27.7 %all-to-all-done = bf16[16,3,24576]{2,1,0:T(4,128)(2,1)S(1)} async-done(((bf16[16,3,24576]{2,1,0:T(4,128)(2,1)}), bf16[16,3,24576]{2,1,0:T(4,128)(2,1)S(1)}, u32[]{:S(2)}, u32[]{:S(2)}) %all-to-all-start) | async-done | bytes 2359328 | tf_op jit(solution)/shard_map/all_to_all | solution.py:107
  164.5 147.7 %while.14 = (s32[]{:T(128)}, bf16[8,6,24576]{2,1,0:T(8,128)(2,1)}, f32[8,192,768]{2,1,0:T(8,128)}, f32[8,768,192]{1,2,0:T(8,128)}, bf16[8,6,24576]{2,1,0:T(8,128...) while((s32[]{:T(128)}, bf16[8,6,24576]{2,1,0:T(8,128)(2,1)}, ...), condition=%wide.region_5.6_spmd, body=%wide.region_4.5_spmd.sunk | while | flops 1176846336 | bytes 16123001 | solution.py:110
  166.4 7.3 fusion.141
  178.2 3.9 fusion.142
  184.8 7.3 fusion.141
  196.5 3.9 fusion.142
  203.2 7.3 fusion.141
  215.0 3.9 fusion.142
  221.6 7.3 fusion.141
  233.4 3.9 fusion.142
  240.0 7.3 fusion.141
  251.8 3.9 fusion.142
  258.4 7.3 fusion.141
  270.2 3.9 fusion.142
  276.8 7.3 fusion.141
  288.6 3.9 fusion.142
  295.2 7.3 fusion.141
  307.0 3.9 fusion.142
  316.8 6.8 all-to-all-start.2
  326.6 22.0 %all-to-all-done.2 = bf16[8,6,24576]{2,0,1:T(8,128)(2,1)} async-done(((bf16[8,6,24576]{2,0,1:T(8,128)(2,1)}), bf16[8,6,24576]{2,0,1:T(8,128)(2,1)}, u32[]{:S(2)}, u32[]{:S(2)}) %all-to-all-start.2) | async-done | bytes 2359328 | tf_op jit(solution)/shard_map/all_to_all | solution.py:111
  348.6 3.7 copy.29
  357.6 3.3 reshape.266
  360.9 4.0 add_convert_fusion
  367.2 1250.3 %all-reduce.4.cloned.1.call-done = (f32[8,192,768]{2,1,0:T(8,128)}, f32[8,768,192]{1,2,0:T(8,128)}) async-done(((f32[8,192,768]{2,1,0:T(8,128)}, f32[8,768,192]{1,2,0:T(8,128)}), (f32[8,192,768]{2,1,0:T(8,128)}, f32[8,768,192]{1,2,0:T(8,128)})) %all-reduce.4.cloned.1.call-update) | async-done | bytes 9437200 | tf_op jit(solution)/shard_map/psum | solution.py:112
  1617.5 5.0 copy.60
  (130 shorter events, 113.5 us)
Async XLA Ops:
  7.2 60.3 %copy-start = (bf16[768,192]{0,1:T(8,128)(2,1)S(1)}, bf16[768,192]{0,1:T(8,128)(2,1)}, u32[]{:S(2)}) copy-start(bf16[768,192]{0,1:T(8,128)(2,1)} %param.17) | copy-start | bytes 884740
  9.0 24.0 %collective-permute-start = (bf16[1,3,256,192]{2,3,1,0:T(8,128)(2,1)}, bf16[1,3,256,192]{2,3,1,0:T(8,128)(2,1)S(1)}, u32[]{:S(2)}, u32[]{:S(2)}) collective-permute-start(bf16[1,3,256,192]{2,3,1,0:T(8,128)(2,1)} %get-tuple-element.88), channel_id=1, source_target_pairs={{0,128},{1,129},{2,130},{3,131},{4,132},{5,133},{6,134},{7,135},{8... | collective-permute-start | bytes 884744 | tf_op jit(solution)/shard_map/ppermute | solution.py:16
  13.1 22.7 %collective-permute-start.1 = (bf16[1,3,256,192]{2,3,1,0:T(8,128)(2,1)S(1)}, bf16[1,3,256,192]{2,3,1,0:T(8,128)(2,1)S(1)}, u32[]{:S(2)}, u32[]{:S(2)}) collective-permute-start(bf16[1,3,256,192]{2,3,1,0:T(8,128)(2,1)S(1)} %get-tuple-element.89), channel_id=1, source_target_pairs={{128,0},{129,1},{130,2},{131,3},{132,4},{133,5},{134,6},{135,7},{1... | collective-permute-start | bytes 884744 | tf_op jit(solution)/shard_map/ppermute | solution.py:19
  26.1 6.8 copy-start.6
  26.1 6.9 copy-start.2
  26.1 95.2 %all-to-all-start.1 = ((bf16[16,3,24576]{2,1,0:T(4,128)(2,1)}), bf16[16,3,24576]{2,1,0:T(4,128)(2,1)}, u32[]{:S(2)}, u32[]{:S(2)}) async-start(bf16[16,3,24576]{2,1,0:T(4,128)(2,1)} %reshape.262), calls=%async_computation.1 | async-start | bytes 6291456 | tf_op jit(solution)/shard_map/all_to_all | solution.py:108
  64.9 0.7 copy-start.7
  65.6 2.4 copy-start.4
  121.4 38.3 %all-to-all-start = ((bf16[16,3,24576]{2,1,0:T(4,128)(2,1)}), bf16[16,3,24576]{2,1,0:T(4,128)(2,1)S(1)}, u32[]{:S(2)}, u32[]{:S(2)}) async-start(bf16[16,3,24576]{2,1,0:T(4,128)(2,1)} %reshape.260), calls=%async_computation | async-start | bytes 6291456 | tf_op jit(solution)/shard_map/all_to_all | solution.py:107
  125.3 1492.2 %all-reduce.4.cloned.1.call-start = ((), (), s32[]{:S(2)}) async-start(), calls=%async_computation.3 | async-start | bytes 18874368 | tf_op jit(solution)/shard_map/psum | solution.py:112
  312.2 1.9 copy-start.5
  316.8 6.8 copy-start.3
  316.8 31.9 %all-to-all-start.2 = ((bf16[8,6,24576]{2,0,1:T(8,128)(2,1)}), bf16[8,6,24576]{2,0,1:T(8,128)(2,1)}, u32[]{:S(2)}, u32[]{:S(2)}) async-start(bf16[8,6,24576]{2,0,1:T(8,128)(2,1)} %copy.28), calls=%async_computation.2 | async-start | bytes 4718592 | tf_op jit(solution)/shard_map/all_to_all | solution.py:111
  1617.5 5.0 slice-start
  1617.5 5.0 slice-start.1
  1617.5 7.2 copy-start.1
Sparse Core Ops, SparseCore 0:
  312.3 1305.1 all-reduce.3
where the time goes:
time: 1640 us; the launch traced here: 1630 us
  waiting for transfers between devices  1300 us (79%)
  matrix products  161 us (10%)
  local copies, waits for them, and re-layouts  98.1 us (6%)
  other arithmetic  35 us (2%)
  starting transfers between devices  22.9 us (1%)
    psum x1, waiting for transfers between devices, body(): grad_in, grad_out = lax.psum((grad_in, grad_out), ('lat', 'dp'))  1250 us
    dot_general x8, matrix products, expert_pass(): pre_act = jnp.dot(inputs, w_in, preferred_element_type=jnp.float32)  58.5 us
    dot_general x1, matrix products, dense_block(): reduced = jnp.dot(active, w_reduce, preferred_element_type=jnp.float32)  42.4 us
  transfers between devices with their start and end apart: 6, of which 3 were waited for; matrix products, arithmetic and copies ran while one was open for 8% of the time, Pallas kernels for 0%

commit v1 on v0

--- a/solution.py
+++ b/solution.py
@@ -109,7 +109,7 @@
     )
     results, grad_in, grad_out = lax.map(run_expert, (arrived, arrived_grads, exp_in, exp_out))
     returned = lax.all_to_all(results, "exp", split_axis=1, concat_axis=0, tiled=True)
-    grad_in, grad_out = lax.psum((grad_in, grad_out), ("lat", "dp"))
+    grad_in, grad_out = lax.psum(lax.psum((grad_in, grad_out), "dp"), "lat")
     expert_out = jnp.dot(
         placer.T, returned.reshape(EXPERTS * CAP, block_width), preferred_element_type=jnp.float32
     ).astype(jnp.bfloat16)

time: 1640 us -> 802 us (0.49)
  waiting for transfers between devices: 1300 us -> 460 us
    psum x1 -> x2, waiting for transfers between devices: 1250 us -> 389 us  [body(): grad_in, grad_out = lax.psum(lax.psum((grad_in, grad_out), 'dp'), 'lat')]
    all_to_all x1, waiting for transfers between devices: 22 us -> 42.6 us  [body(): lax.all_to_all(results, 'exp', split_axis=1, concat_axis=0, tiled=True)]
  transfers between devices with their start and end apart: 6 -> 7, of which waited for: 3 -> 4; matrix products, arithmetic and copies ran while one was open for 8% -> 17% of each run, Pallas kernels for 0% -> 0%
where the time goes in v1:
time: 802 us; the launch traced here: 792 us
  waiting for transfers between devices  460 us (57%)
  matrix products  161 us (20%)
  local copies, waits for them, and re-layouts  101 us (13%)
  other arithmetic  35.4 us (4%)
  starting transfers between devices  20.5 us (3%)
  between operations  14.5 us (2%)
    psum x2, waiting for transfers between devices, body(): grad_in, grad_out = lax.psum(lax.psum((grad_in, grad_out), 'dp'), 'lat')  389 us
    dot_general x8, matrix products, expert_pass(): pre_act = jnp.dot(inputs, w_in, preferred_element_type=jnp.float32)  58.7 us
    all_to_all x1, waiting for transfers between devices, body(): lax.all_to_all(results, 'exp', split_axis=1, concat_axis=0, tiled=True)  42.6 us
    dot_general x1, matrix products, dense_block(): reduced = jnp.dot(active, w_reduce, preferred_element_type=jnp.float32)  42.4 us
    dot_general x8, matrix products, expert_pass(): grad_in = jnp.dot(inputs.T, scaled, preferred_element_type=jnp.float32)  31 us
    all_to_all x1, waiting for transfers between devices, body(): lax.all_to_all(outgoing, 'exp', split_axis=0, concat_axis=1, tiled=True)  27.7 us
    reduce_sum x1, other arithmetic, dense_block(): channel_mean = jnp.mean(smoothed, axis=-1, keepdims=True)  26.9 us
    dynamic_slice x16, local copies, waits for them, and re-layouts, body(): lax.map(run_expert, (arrived, arrived_grads, exp_in, exp_out))  22.6 us
  transfers between devices with their start and end apart: 7, of which 4 were waited for; matrix products, arithmetic and copies ran while one was open for 17% of the time, Pallas kernels for 0%

profile of v1, /device:TPU:2, one launch (start us, length us, event | category | flops | bytes accessed | tf_op | source)
XLA Modules:
  0.0 791.9 jit_solution(1799531077816769084)
XLA Ops:
  9.0 4.0 collective-permute-start
  26.1 6.8 all-to-all-start.1
  38.0 26.9 %fusion.104 = (f32[16,256]{1,0:T(8,128)S(1)}, f32[1,16,256,192]{2,3,1,0:T(8,128)S(1)}) fusion(f32[192]{0:T(256)S(1)} %bitcast.171, bf16[1,22,262,192]{2,3,1,0:T(8,128)(2,1)S(1)} %fusion.69, f32[192]{0:T(256)S(1)} %bitcast.172, f32[192]{0:T(256)S(1)} %bitcast.144, f32[192]{0:T(256)S(1)} %bitcast.145, ...), kind=kLoop, calls=%fused_computation.138 | loop fusion | flops 115601408 | bytes 80270080 | tf_op jit(solution)/shard_map/reduce_sum | solution.py:48
  68.0 42.4 %fusion.60 = bf16[4096,192]{0,1:T(8,128)(2,1)} fusion(f32[4096,192]{0,1:T(8,128)S(1)} %bitcast.141, bf16[768,192]{0,1:T(8,128)(2,1)S(1)} %copy-done, bf16[4096,192]{0,1:T(8,128)(2,1)} %bitcast.142, bf16[192,768]{1,0:T(8,128)(2,1)} %param.16), kind=kOutput, calls=%fused_computation.83 | convolution fusion | flops 2621964288 | bytes 6881280 | tf_op jit(solution)/shard_map/dot_general | solution.py:55
  121.4 4.0 all-to-all-start
  125.4 3.6 copy.25
  132.0 27.7 %all-to-all-done = bf16[16,3,24576]{2,1,0:T(4,128)(2,1)S(1)} async-done(((bf16[16,3,24576]{2,1,0:T(4,128)(2,1)}), bf16[16,3,24576]{2,1,0:T(4,128)(2,1)S(1)}, u32[]{:S(2)}, u32[]{:S(2)}) %all-to-all-start) | async-done | bytes 2359328 | tf_op jit(solution)/shard_map/all_to_all | solution.py:107
  164.4 147.8 %while.14 = (s32[]{:T(128)}, bf16[8,6,24576]{2,1,0:T(8,128)(2,1)}, f32[8,192,768]{2,1,0:T(8,128)}, f32[8,768,192]{1,2,0:T(8,128)}, bf16[8,6,24576]{2,1,0:T(8,128...) while((s32[]{:T(128)}, bf16[8,6,24576]{2,1,0:T(8,128)(2,1)}, ...), condition=%wide.region_5.6_spmd, body=%wide.region_4.5_spmd.sunk | while | flops 1176846336 | bytes 16123001 | solution.py:110
  166.3 7.3 fusion.141
  178.1 3.9 fusion.142
  184.8 7.3 fusion.141
  196.6 3.9 fusion.142
  203.2 7.3 fusion.141
  215.0 3.9 fusion.142
  221.6 7.3 fusion.141
  233.4 3.9 fusion.142
  240.0 7.3 fusion.141
  251.8 3.9 fusion.142
  258.4 7.3 fusion.141
  270.2 3.9 fusion.142
  276.9 7.3 fusion.141
  288.7 3.9 fusion.142
  295.3 7.3 fusion.141
  307.1 3.9 fusion.142
  312.3 212.8 %all-reduce.6.cloned.1.call-done = (f32[8,192,768]{2,1,0:T(8,128)}, f32[8,768,192]{1,2,0:T(8,128)}) async-done(((f32[8,192,768]{2,1,0:T(8,128)}, f32[8,768,192]{1,2,0:T(8,128)}), (f32[8,192,768]{2,1,0:T(8,128)}, f32[8,768,192]{1,2,0:T(8,128)})) %all-reduce.6.cloned.1.call-update) | async-done | bytes 9437200 | tf_op jit(solution)/shard_map/psum | solution.py:112
  529.7 4.4 all-to-all-start.2
  534.0 4.2 copy.32
  538.2 42.6 %all-to-all-done.2 = bf16[8,6,24576]{2,0,1:T(8,128)(2,1)S(1)} async-done(((bf16[8,6,24576]{2,0,1:T(8,128)(2,1)}), bf16[8,6,24576]{2,0,1:T(8,128)(2,1)S(1)}, u32[]{:S(2)}, u32[]{:S(2)}) %all-to-all-start.2) | async-done | bytes 2359328 | tf_op jit(solution)/shard_map/all_to_all | solution.py:111
  582.2 3.7 copy.29
  594.4 4.4 add_convert_fusion
  601.1 176.6 %all-reduce.8.cloned.1.call-done = (f32[8,192,768]{2,1,0:T(8,128)}, f32[8,768,192]{1,2,0:T(8,128)}) async-done(((f32[8,192,768]{2,1,0:T(8,128)}, f32[8,768,192]{1,2,0:T(8,128)}), (f32[8,192,768]{2,1,0:T(8,128)}, f32[8,768,192]{1,2,0:T(8,128)})) %all-reduce.8.cloned.1.call-update) | async-done | bytes 9437200 | tf_op jit(solution)/shard_map/psum | solution.py:112
  777.7 5.0 copy.62
  (133 shorter events, 118.2 us)
Async XLA Ops:
  7.2 60.3 %copy-start = (bf16[768,192]{0,1:T(8,128)(2,1)S(1)}, bf16[768,192]{0,1:T(8,128)(2,1)}, u32[]{:S(2)}) copy-start(bf16[768,192]{0,1:T(8,128)(2,1)} %param.17) | copy-start | bytes 884740
  9.0 23.9 %collective-permute-start = (bf16[1,3,256,192]{2,3,1,0:T(8,128)(2,1)}, bf16[1,3,256,192]{2,3,1,0:T(8,128)(2,1)S(1)}, u32[]{:S(2)}, u32[]{:S(2)}) collective-permute-start(bf16[1,3,256,192]{2,3,1,0:T(8,128)(2,1)} %get-tuple-element.90), channel_id=1, source_target_pairs={{0,128},{1,129},{2,130},{3,131},{4,132},{5,133},{6,134},{7,135},{8... | collective-permute-start | bytes 884744 | tf_op jit(solution)/shard_map/ppermute | solution.py:16
  13.1 22.6 %collective-permute-start.1 = (bf16[1,3,256,192]{2,3,1,0:T(8,128)(2,1)S(1)}, bf16[1,3,256,192]{2,3,1,0:T(8,128)(2,1)S(1)}, u32[]{:S(2)}, u32[]{:S(2)}) collective-permute-start(bf16[1,3,256,192]{2,3,1,0:T(8,128)(2,1)S(1)} %get-tuple-element.91), channel_id=1, source_target_pairs={{128,0},{129,1},{130,2},{131,3},{132,4},{133,5},{134,6},{135,7},{1... | collective-permute-start | bytes 884744 | tf_op jit(solution)/shard_map/ppermute | solution.py:19
  26.1 6.8 copy-start.6
  26.1 6.9 copy-start.2
  26.1 95.3 %all-to-all-start.1 = ((bf16[16,3,24576]{2,1,0:T(4,128)(2,1)}), bf16[16,3,24576]{2,1,0:T(4,128)(2,1)}, u32[]{:S(2)}, u32[]{:S(2)}) async-start(bf16[16,3,24576]{2,1,0:T(4,128)(2,1)} %reshape.262), calls=%async_computation.1 | async-start | bytes 6291456 | tf_op jit(solution)/shard_map/all_to_all | solution.py:108
  64.9 0.7 copy-start.7
  65.6 2.4 copy-start.4
  121.4 38.3 %all-to-all-start = ((bf16[16,3,24576]{2,1,0:T(4,128)(2,1)}), bf16[16,3,24576]{2,1,0:T(4,128)(2,1)S(1)}, u32[]{:S(2)}, u32[]{:S(2)}) async-start(bf16[16,3,24576]{2,1,0:T(4,128)(2,1)} %reshape.260), calls=%async_computation | async-start | bytes 6291456 | tf_op jit(solution)/shard_map/all_to_all | solution.py:107
  125.4 399.7 %all-reduce.6.cloned.1.call-start = ((), (), s32[]{:S(2)}) async-start(), calls=%async_computation.3 | async-start | bytes 18874368 | tf_op jit(solution)/shard_map/psum | solution.py:112
  312.2 465.5 %all-reduce.8.cloned.1.call-start = ((), (), s32[]{:S(2)}) async-start(), calls=%async_computation.4 | async-start | bytes 18874368 | tf_op jit(solution)/shard_map/psum | solution.py:112
  525.1 1.9 copy-start.5
  529.7 51.2 %all-to-all-start.2 = ((bf16[8,6,24576]{2,0,1:T(8,128)(2,1)}), bf16[8,6,24576]{2,0,1:T(8,128)(2,1)S(1)}, u32[]{:S(2)}, u32[]{:S(2)}) async-start(bf16[8,6,24576]{2,0,1:T(8,128)(2,1)} %copy.28), calls=%async_computation.2 | async-start | bytes 4718592 | tf_op jit(solution)/shard_map/all_to_all | solution.py:111
  580.8 1.4 copy-start.3
  777.7 5.0 slice-start
  777.7 5.0 slice-start.1
  777.7 7.2 copy-start.1
Sparse Core Ops, SparseCore 0:
  312.4 212.6 all-reduce.5
  528.1 249.5 all-reduce.7
